TPU v7x, 32 devices: a whole 2x2x4 slice. The times are simulated.
32 devices in a mesh: groups: 2 (over y), wide: 4 (over z), narrow: 2 (over x), inner: 2 (over core).
Axes of the slice: x: 2, y: 2, z: 4, core: 2. Of those that a mesh axis runs over, the one named last changes fastest.
Arguments:
- tokens: bfloat16 [128, 6144], P(('groups', 'wide'), ('narrow', 'inner')), parts along dimension 0, may hold values from -6 to 6
- cotangent: bfloat16 [128, 6144], P(('groups', 'wide'), ('narrow', 'inner')), parts along dimension 0, may hold values from -3 to 3
- w_gate: bfloat16 [6144, 16384], P(('narrow', 'inner'), 'wide'), may hold values from -0.078125 to 0.078125
- w_up: bfloat16 [6144, 16384], P(('narrow', 'inner'), 'wide'), may hold values from -0.078125 to 0.078125
- w_down: bfloat16 [16384, 6144], P('wide', ('narrow', 'inner')), may hold values from -0.046875 to 0.046875
Outputs:
- output: bfloat16 [128, 6144], P(('groups', 'wide'), ('narrow', 'inner')), parts along dimension 0
- grad_input: bfloat16 [128, 6144], P(('groups', 'wide'), ('narrow', 'inner')), parts along dimension 0
- grad_wgate: bfloat16 [12288, 16384], P(('groups', 'narrow', 'inner'), 'wide'), parts along dimension 0
- grad_wup: bfloat16 [12288, 16384], P(('groups', 'narrow', 'inner'), 'wide'), parts along dimension 0
- grad_wdown: bfloat16 [32768, 6144], P(('groups', 'wide'), ('narrow', 'inner')), parts along dimension 0
There are 2 independent parts, one for each index of `groups`. A program takes and returns all parts, laid end to end along the dimension named above; an argument that names none is the same for every part. Nothing has to cross between parts.
All inputs are finite; a program needn't handle non-finite values.
Results may differ from a plain program's by a relative error of at most 0.012.
Values may be sent and summed in bfloat16 or wider, within the bound.
No kernel may reach another device: no remote copies, remote signals or barrier semaphores. Data moves between devices by JAX's collectives and lax.ppermute only.
A program may use at most 192 MiB of HBM per device.

v0:
```python
import jax
import jax.numpy as jnp
from jax import lax
from jax.sharding import PartitionSpec as P


def contract_last(left, right):
    return lax.dot_general(
        left, right, (((1,), (1,)), ((), ())), preferred_element_type=jnp.float32
    )


def contract_first(left, right):
    return lax.dot_general(
        left, right, (((0,), (0,)), ((), ())), preferred_element_type=jnp.float32
    )


def activate(gate, up):
    return (gate * jax.nn.sigmoid(gate) * up).astype(jnp.bfloat16)


def grad_parts(gate, up, upstream):
    sigmoid_gate = jax.nn.sigmoid(gate)
    grad_gate = (upstream * up * sigmoid_gate * (1.0 + gate * (1.0 - sigmoid_gate))).astype(
        jnp.bfloat16
    )
    grad_up = (upstream * gate * sigmoid_gate).astype(jnp.bfloat16)
    return (grad_gate, grad_up)


def body(tokens, cotangent, w_gate, w_up, w_down):
    gathered = lax.all_gather(tokens, "wide", axis=0, tiled=True)
    gate_part = jnp.dot(gathered, w_gate, preferred_element_type=jnp.float32)
    up_part = jnp.dot(gathered, w_up, preferred_element_type=jnp.float32)
    gate, up = lax.psum((gate_part, up_part), ("narrow", "inner"))
    hidden = activate(gate, up)
    output = lax.psum_scatter(
        jnp.dot(hidden, w_down, preferred_element_type=jnp.float32).astype(jnp.bfloat16),
        "wide",
        scatter_dimension=0,
        tiled=True,
    )
    cot_all = lax.all_gather(cotangent, "wide", axis=0, tiled=True)
    upstream_part = contract_last(cot_all, w_down)
    grad_wdown = contract_first(hidden, cot_all).astype(jnp.bfloat16)
    upstream = lax.psum(upstream_part, ("narrow", "inner"))
    grad_gate, grad_up = grad_parts(gate, up, upstream)
    grad_input = lax.psum_scatter(
        (contract_last(grad_gate, w_gate) + contract_last(grad_up, w_up)).astype(jnp.bfloat16),
        "wide",
        scatter_dimension=0,
        tiled=True,
    )
    grad_wgate = contract_first(gathered, grad_gate).astype(jnp.bfloat16)
    grad_wup = contract_first(gathered, grad_up).astype(jnp.bfloat16)
    return (output, grad_input, grad_wgate, grad_wup, grad_wdown)


def solution(mesh):
    return jax.shard_map(
        body,
        mesh=mesh,
        in_specs=(
            P(("groups", "wide"), ("narrow", "inner")),
            P(("groups", "wide"), ("narrow", "inner")),
            P(("narrow", "inner"), "wide"),
            P(("narrow", "inner"), "wide"),
            P("wide", ("narrow", "inner")),
        ),
        out_specs=(
            P(("groups", "wide"), ("narrow", "inner")),
            P(("groups", "wide"), ("narrow", "inner")),
            P(("groups", "narrow", "inner"), "wide"),
            P(("groups", "narrow", "inner"), "wide"),
            P(("groups", "wide"), ("narrow", "inner")),
        ),
        check_vma=False,
    )
```

profile of v0, /device:TPU:0, one launch (start us, length us, event | category | flops | bytes accessed | tf_op | source)
XLA Modules:
  0.0 206.2 jit_solution(17270711638761119251)
XLA Ops:
  7.2 0.0 all-reduce.3.cloned.1.call-start
  7.2 0.0 copy-start
  7.2 15.8 %all_gather.6 = bf16[64,1536]{1,0:T(8,128)(2,1)S(1)} all-gather(bf16[16,1536]{1,0:T(8,128)(2,1)} %param.5), channel_id=1, replica_groups=mesh['groups'=2,'wide'=4,'narrow'=2,'inner'=2] {'wide'}, dimensions={0}, use_global_device_ids=true | all-gather | bytes 245760 | tf_op jit(solution)/shard_map/all_gather | solution.py:33
  23.0 0.0 slice-start
  23.0 0.0 slice-start.1
  23.0 8.0 %fusion.4 = f32[64,4096]{1,0:T(8,128)} fusion(bf16[64,1536]{1,0:T(8,128)(2,1)S(1)} %all_gather.6, bf16[1536,4096]{1,0:T(8,128)(2,1)} %param.8), kind=kOutput, calls=%fused_computation.13 | convolution fusion | flops 805306368 | bytes 13828096 | tf_op jit(solution)/shard_map/dot_general | solution.py:35
  31.0 0.0 copy-done
  31.0 0.0 copy-start.1
  31.0 0.0 slice-start.2
  31.0 3.3 %fusion.3 = f32[64,4096]{1,0:T(8,128)} fusion(bf16[64,1536]{1,0:T(8,128)(2,1)S(1)} %all_gather.6, bf16[1536,4096]{1,0:T(8,128)(2,1)S(1)} %copy-done), kind=kOutput, calls=%fused_computation.12 | convolution fusion | flops 805306368 | bytes 13828096 | tf_op jit(solution)/shard_map/dot_general | solution.py:34
  34.3 0.0 copy-done.1
  34.3 14.0 %all_gather.7 = bf16[64,1536]{1,0:T(8,128)(2,1)S(1)} all-gather(bf16[16,1536]{1,0:T(8,128)(2,1)S(1)} %copy-done.1), channel_id=1, replica_groups=mesh['groups'=2,'wide'=4,'narrow'=2,'inner'=2] {'wide'}, dimensions={0}, use_global_device_ids=true | all-gather | bytes 245760 | tf_op jit(solution)/shard_map/all_gather | solution.py:44
  48.3 0.0 slice-done
  48.3 0.0 slice-done.1
  48.3 0.0 slice-done.2
  48.3 4.9 %fusion.5 = f32[64,4096]{1,0:T(8,128)} fusion(bf16[64,1536]{1,0:T(8,128)(2,1)S(1)} %all_gather.7, bf16[4096,1536]{1,0:T(8,128)(2,1)S(1)} %bitcast.23), kind=kOutput, calls=%fused_computation.14 | convolution fusion | flops 805306368 | bytes 13828096 | tf_op jit(solution)/shard_map/dot_general | solution.py:8
  53.2 0.0 all-reduce.3.cloned.1.call-update
  53.2 0.0 reduce-scatter.3.cloned.1.call-start
  53.3 69.9 %all-reduce.3.cloned.1.call-done = (f32[64,4096]{1,0:T(8,128)}, f32[64,4096]{1,0:T(8,128)}, f32[64,4096]{1,0:T(8,128)}) async-done(((f32[64,4096]{1,0:T(8,128)}, f32[64,4096]{1,0:T(8,128)}, f32[64,4096]{1,0:T(8,128)}), (f32[64,4096]{1,0:T(8,128)}, f32[64,4096]{1,0:T(8,128)}, f32[64,4096]{1,0:T(8,128)})) %all-reduce.3.cloned.1.call-update) | async-done | bytes 3145744 | tf_op jit(solution)/shard_map/psum | solution.py:36
  123.2 2.4 %multiply_convert_fusion = (bf16[64,4096]{1,0:T(8,128)(2,1)S(1)}, bf16[64,4096]{1,0:T(8,128)(2,1)S(1)}, bf16[64,4096]{1,0:T(8,128)(2,1)S(1)}) fusion(f32[64,4096]{1,0:T(8,128)} %get-tuple-element.12, f32[64,4096]{1,0:T(8,128)} %get-tuple-element.11, f32[64,4096]{1,0:T(8,128)} %get-tuple-element.10), kind=kLoop, calls=%fused_computation.8 | loop fusion | flops 4194304 | bytes 4718592 | tf_op jit(solution)/shard_map/convert_element_type | solution.py:28
  125.6 0.0 slice-start.3
  125.6 0.0 slice-start.4
  125.6 8.7 %fusion.6 = f32[64,1536]{1,0:T(8,128)S(1)} fusion(bf16[64,4096]{1,0:T(8,128)(2,1)S(1)} %get-tuple-element.14, bf16[1536,4096]{1,0:T(8,128)(2,1)} %param.7), kind=kOutput, calls=%fused_computation.15 | convolution fusion | flops 805306368 | bytes 13500416 | tf_op jit(solution)/shard_map/dot_general | solution.py:8
  134.3 0.0 slice-start.5
  134.3 6.6 %fusion = bf16[1536,4096]{0,1:T(8,128)(2,1)} fusion(bf16[64,4096]{1,0:T(8,128)(2,1)S(1)} %get-tuple-element.14, bf16[64,1536]{1,0:T(8,128)(2,1)S(1)} %all_gather.6), kind=kOutput, calls=%fused_computation.3 | convolution fusion | flops 811597824 | bytes 13303808 | tf_op jit(solution)/shard_map/dot_general | solution.py:14
  140.9 0.0 slice-done.3
  140.9 0.0 slice-done.4
  140.9 0.0 slice-done.5
  141.0 3.0 %convolution_convert_fusion.3 = bf16[64,1536]{1,0:T(8,128)(2,1)} fusion(bf16[64,4096]{1,0:T(8,128)(2,1)S(1)} %get-tuple-element.15, bf16[4096,1536]{1,0:T(8,128)(2,1)S(1)} %bitcast.25), kind=kOutput, calls=%fused_computation.7 | convolution fusion | flops 805404672 | bytes 13303808 | tf_op jit(solution)/shard_map/dot_general | solution.py:39
  143.9 0.0 reduce-scatter.3.cloned.1.call-update
  144.0 0.2 reduce-scatter.5.cloned.1.call-start
  144.2 6.4 %fusion.1 = bf16[1536,4096]{0,1:T(8,128)(2,1)} fusion(bf16[64,4096]{1,0:T(8,128)(2,1)S(1)} %get-tuple-element.13, bf16[64,1536]{1,0:T(8,128)(2,1)S(1)} %all_gather.6), kind=kOutput, calls=%fused_computation.4 | convolution fusion | flops 811597824 | bytes 13303808 | tf_op jit(solution)/shard_map/dot_general | solution.py:14
  150.6 9.2 %fusion.2 = bf16[64,1536]{1,0:T(8,128)(2,1)} fusion(f32[64,1536]{1,0:T(8,128)S(1)} %fusion.6, bf16[64,4096]{1,0:T(8,128)(2,1)S(1)} %get-tuple-element.13, bf16[1536,4096]{1,0:T(8,128)(2,1)} %param.8), kind=kOutput, calls=%fused_computation.6 | convolution fusion | flops 805502976 | bytes 13697024 | tf_op jit(solution)/shard_map/dot_general | solution.py:8
  159.8 0.0 reduce-scatter.5.cloned.1.call-update
  159.8 6.6 %convolution_convert_fusion = bf16[4096,1536]{1,0:T(8,128)(2,1)} fusion(bf16[64,4096]{1,0:T(8,128)(2,1)S(1)} %get-tuple-element.15, bf16[64,1536]{1,0:T(8,128)(2,1)S(1)} %all_gather.7), kind=kOutput, calls=%fused_computation | convolution fusion | flops 811597824 | bytes 13303808 | tf_op jit(solution)/shard_map/dot_general | solution.py:14
  166.4 16.6 %copy.10 = bf16[1536,4096]{1,0:T(8,128)(2,1)} copy(bf16[1536,4096]{0,1:T(8,128)(2,1)} %fusion) | data formatting | bytes 25165824
  183.0 16.6 %copy.11 = bf16[1536,4096]{1,0:T(8,128)(2,1)} copy(bf16[1536,4096]{0,1:T(8,128)(2,1)} %fusion.1) | data formatting | bytes 25165824
  199.6 0.0 reduce-scatter.3.cloned.1.call-done
  199.6 0.0 reduce-scatter.5.cloned.1.call-done
  (2 shorter events, 0.0 us)
Async XLA Ops:
  7.2 116.0 %all-reduce.3.cloned.1.call-start = ((), (), s32[]{:S(2)}) async-start(), calls=%async_computation.4 | async-start | bytes 6291456 | tf_op jit(solution)/shard_map/psum | solution.py:36
  7.2 23.8 %copy-start = (bf16[1536,4096]{1,0:T(8,128)(2,1)S(1)}, bf16[1536,4096]{1,0:T(8,128)(2,1)}, u32[]{:S(2)}) copy-start(bf16[1536,4096]{1,0:T(8,128)(2,1)} %param.7) | copy-start | bytes 37748740
  23.0 25.3 %slice-start = ((s8[12582912]{0:T(1024)(128)(4,1)}), s8[4194304]{0:T(1024)(128)(4,1)S(1)}, s32[]{:S(2)}) async-start(s8[12582912]{0:T(1024)(128)(4,1)} %bitcast.22), calls=%async_computation.5 | async-start | bytes 8388608
  23.0 25.3 %slice-start.1 = ((s8[12582912]{0:T(1024)(128)(4,1)}), s8[4194304]{0:T(1024)(128)(4,1)S(1)}, s32[]{:S(2)}) async-start(s8[12582912]{0:T(1024)(128)(4,1)} %bitcast.22), calls=%async_computation.6 | async-start | bytes 8388608
  31.0 3.3 %copy-start.1 = (bf16[16,1536]{1,0:T(8,128)(2,1)S(1)}, bf16[16,1536]{1,0:T(8,128)(2,1)}, u32[]{:S(2)}) copy-start(bf16[16,1536]{1,0:T(8,128)(2,1)} %param.6) | copy-start | bytes 147460
  31.0 17.3 %slice-start.2 = ((s8[12582912]{0:T(1024)(128)(4,1)}), s8[4194304]{0:T(1024)(128)(4,1)S(1)}, s32[]{:S(2)}) async-start(s8[12582912]{0:T(1024)(128)(4,1)} %bitcast.22), calls=%async_computation.7 | async-start | bytes 8388608
  53.2 146.4 %reduce-scatter.3.cloned.1.call-start = ((), (), s32[]{:S(2)}) async-start(), calls=%async_computation.2 | async-start | bytes 245760 | tf_op jit(solution)/shard_map/reduce_scatter | solution.py:38
  125.6 15.3 %slice-start.3 = ((s8[12582912]{0:T(1024)(128)(4,1)}), s8[4194304]{0:T(1024)(128)(4,1)S(1)}, s32[]{:S(2)}) async-start(s8[12582912]{0:T(1024)(128)(4,1)} %bitcast.24), calls=%async_computation.8 | async-start | bytes 8388608
  125.6 15.3 %slice-start.4 = ((s8[12582912]{0:T(1024)(128)(4,1)}), s8[4194304]{0:T(1024)(128)(4,1)S(1)}, s32[]{:S(2)}) async-start(s8[12582912]{0:T(1024)(128)(4,1)} %bitcast.24), calls=%async_computation.9 | async-start | bytes 8388608
  134.3 6.6 %slice-start.5 = ((s8[12582912]{0:T(1024)(128)(4,1)}), s8[4194304]{0:T(1024)(128)(4,1)S(1)}, s32[]{:S(2)}) async-start(s8[12582912]{0:T(1024)(128)(4,1)} %bitcast.24), calls=%async_computation.10 | async-start | bytes 8388608
  144.0 55.7 %reduce-scatter.5.cloned.1.call-start = ((), (), s32[]{:S(2)}) async-start(), calls=%async_computation.3 | async-start | bytes 245760 | tf_op jit(solution)/shard_map/reduce_scatter | solution.py:49
Sparse Core Ops, SparseCore 0:
  53.3 69.8 all-reduce.2
  144.1 19.4 reduce-scatter.2
  166.5 17.5 reduce-scatter.4
where the time goes:
time: 207 us; the launch traced here: 206 us
  waiting for transfers between devices  70 us (34%)
  matrix products  56.6 us (27%)
  local copies, waits for them, and re-layouts  33.3 us (16%)
  blocking collectives  29.8 us (14%)
  between operations  13.8 us (7%)
  other arithmetic  2.4 us (1%)
    psum x1, waiting for transfers between devices, body(): gate, up = lax.psum((gate_part, up_part), ('narrow', 'inner'))  69.9 us
    unnamed x18, local copies, waits for them, and re-layouts  33.3 us
    dot_general x3, matrix products, contract_last(): lax.dot_general(left, right, (((1,), (1,)), ((), ())), preferred_element_...  22.7 us
    dot_general x3, matrix products, contract_first(): lax.dot_general(left, right, (((0,), (0,)), ((), ())), preferred_element_...  19.7 us
    all_gather x1, blocking collectives, body(): gathered = lax.all_gather(tokens, 'wide', axis=0, tiled=True)  15.8 us
    all_gather x1, blocking collectives, body(): cot_all = lax.all_gather(cotangent, 'wide', axis=0, tiled=True)  14 us
    dot_general x1, matrix products, body(): up_part = jnp.dot(gathered, w_up, preferred_element_type=jnp.float32)  7.99 us
  transfers between devices with their start and end apart: 3, of which 1 were waited for; matrix products, arithmetic and copies ran while one was open for 27% of the time, Pallas kernels for 0%

commit v1 on v0

--- a/solution.py
+++ b/solution.py
@@ -33,7 +33,7 @@
     gathered = lax.all_gather(tokens, "wide", axis=0, tiled=True)
     gate_part = jnp.dot(gathered, w_gate, preferred_element_type=jnp.float32)
     up_part = jnp.dot(gathered, w_up, preferred_element_type=jnp.float32)
-    gate, up = lax.psum((gate_part, up_part), ("narrow", "inner"))
+    gate, up = lax.psum(lax.psum((gate_part, up_part), "inner"), "narrow")
     hidden = activate(gate, up)
     output = lax.psum_scatter(
         jnp.dot(hidden, w_down, preferred_element_type=jnp.float32).astype(jnp.bfloat16),

time: 207 us -> 247 us (1.19)
  waiting for transfers between devices: 70 us -> 105 us
  matrix products: 56.6 us -> 61.2 us
    psum x1 -> x3, waiting for transfers between devices: 69.9 us -> 104 us  [the longest x2 65.9 us: body(): gate, up = lax.psum(lax.psum((gate_part, up_part), 'inner'), 'narrow')]
    dot_general x3, matrix products: 22.7 us -> 27.5 us  [contract_last(): lax.dot_general(left, right, (((1,), (1,)), ((), ())), preferred_element_...]
    unnamed x18 -> x12, local copies, waits for them, and re-layouts: 33.3 us -> 33.2 us
  transfers between devices with their start and end apart: 3 -> 5, of which waited for: 1 -> 2; matrix products, arithmetic and copies ran while one was open for 27% -> 26% of each run, Pallas kernels for 0% -> 0%
where the time goes in v1:
time: 247 us; the launch traced here: 246 us
  waiting for transfers between devices  105 us (43%)
  matrix products  61.2 us (25%)
  local copies, waits for them, and re-layouts  33.2 us (13%)
  blocking collectives  29.8 us (12%)
  between operations  13.8 us (6%)
    psum x2, waiting for transfers between devices, body(): gate, up = lax.psum(lax.psum((gate_part, up_part), 'inner'), 'narrow')  65.9 us
    psum x1, waiting for transfers between devices, body(): upstream = lax.psum(upstream_part, ('narrow', 'inner'))  38.3 us
    unnamed x12, local copies, waits for them, and re-layouts  33.2 us
    dot_general x3, matrix products, contract_last(): lax.dot_general(left, right, (((1,), (1,)), ((), ())), preferred_element_...  27.5 us
    dot_general x3, matrix products, contract_first(): lax.dot_general(left, right, (((0,), (0,)), ((), ())), preferred_element_...  19.7 us
    all_gather x1, blocking collectives, body(): gathered = lax.all_gather(tokens, 'wide', axis=0, tiled=True)  15.8 us
    all_gather x1, blocking collectives, body(): cot_all = lax.all_gather(cotangent, 'wide', axis=0, tiled=True)  14 us
    dot_general x1, matrix products, body(): up_part = jnp.dot(gathered, w_up, preferred_element_type=jnp.float32)  7.84 us
  transfers between devices with their start and end apart: 5, of which 2 were waited for; matrix products, arithmetic and copies ran while one was open for 26% of the time, Pallas kernels for 0%

profile of v1, /device:TPU:0, one launch (start us, length us, event | category | flops | bytes accessed | tf_op | source)
XLA Modules:
  0.0 246.1 jit_solution(4538748165556928217)
XLA Ops:
  7.2 0.0 all-reduce.8.cloned.1.call-start
  7.2 0.0 copy-start
  7.2 15.8 %all_gather.6 = bf16[64,1536]{1,0:T(8,128)(2,1)S(1)} all-gather(bf16[16,1536]{1,0:T(8,128)(2,1)} %param.5), channel_id=1, replica_groups=mesh['groups'=2,'wide'=4,'narrow'=2,'inner'=2] {'wide'}, dimensions={0}, use_global_device_ids=true | all-gather | bytes 245760 | tf_op jit(solution)/shard_map/all_gather | solution.py:33
  23.0 7.8 %fusion.4 = f32[64,4096]{1,0:T(8,128)} fusion(bf16[64,1536]{1,0:T(8,128)(2,1)S(1)} %all_gather.6, bf16[1536,4096]{1,0:T(8,128)(2,1)} %param.8), kind=kOutput, calls=%fused_computation.13 | convolution fusion | flops 805306368 | bytes 13828096 | tf_op jit(solution)/shard_map/dot_general | solution.py:35
  30.9 0.0 copy-done
  30.9 0.0 copy-start.1
  30.9 3.3 %fusion.3 = f32[64,4096]{1,0:T(8,128)} fusion(bf16[64,1536]{1,0:T(8,128)(2,1)S(1)} %all_gather.6, bf16[1536,4096]{1,0:T(8,128)(2,1)S(1)} %copy-done), kind=kOutput, calls=%fused_computation.12 | convolution fusion | flops 805306368 | bytes 13828096 | tf_op jit(solution)/shard_map/dot_general | solution.py:34
  34.1 0.0 all-reduce.8.cloned.1.call-update
  34.2 0.0 all-reduce.6.cloned.1.call-start
  34.2 0.0 copy-done.1
  34.2 14.0 %all_gather.7 = bf16[64,1536]{1,0:T(8,128)(2,1)S(1)} all-gather(bf16[16,1536]{1,0:T(8,128)(2,1)S(1)} %copy-done.1), channel_id=1, replica_groups=mesh['groups'=2,'wide'=4,'narrow'=2,'inner'=2] {'wide'}, dimensions={0}, use_global_device_ids=true | all-gather | bytes 245760 | tf_op jit(solution)/shard_map/all_gather | solution.py:44
  48.3 9.6 %fusion.5 = f32[64,4096]{1,0:T(8,128)} fusion(bf16[64,1536]{1,0:T(8,128)(2,1)S(1)} %all_gather.7, bf16[4096,1536]{1,0:T(8,128)(2,1)} %param.9), kind=kOutput, calls=%fused_computation.14 | convolution fusion | flops 805306368 | bytes 13828096 | tf_op jit(solution)/shard_map/dot_general | solution.py:8
  57.9 0.0 all-reduce.6.cloned.1.call-update
  57.9 0.0 all-reduce.10.cloned.1.call-start
  58.0 0.0 all-reduce.8.cloned.1.call-done
  58.0 0.7 all-reduce.10.cloned.1.call-update
  58.7 0.2 reduce-scatter.3.cloned.1.call-start
  58.9 38.3 %all-reduce.6.cloned.1.call-done = f32[64,4096]{1,0:T(8,128)} async-done(((f32[64,4096]{1,0:T(8,128)}), f32[64,4096]{1,0:T(8,128)}) %all-reduce.6.cloned.1.call-update) | async-done | bytes 1048592 | tf_op jit(solution)/shard_map/psum | solution.py:47
  97.2 65.9 %all-reduce.10.cloned.1.call-done = (f32[64,4096]{1,0:T(8,128)}, f32[64,4096]{1,0:T(8,128)}) async-done(((f32[64,4096]{1,0:T(8,128)}, f32[64,4096]{1,0:T(8,128)}), (f32[64,4096]{1,0:T(8,128)}, f32[64,4096]{1,0:T(8,128)})) %all-reduce.10.cloned.1.call-update) | async-done | bytes 2097168 | tf_op jit(solution)/shard_map/psum | solution.py:36
  163.1 2.4 multiply_convert_fusion
  165.5 0.0 slice-start
  165.5 0.0 slice-start.1
  165.5 8.7 %fusion.6 = f32[64,1536]{1,0:T(8,128)S(1)} fusion(bf16[64,4096]{1,0:T(8,128)(2,1)S(1)} %get-tuple-element.15, bf16[1536,4096]{1,0:T(8,128)(2,1)} %param.7), kind=kOutput, calls=%fused_computation.15 | convolution fusion | flops 805306368 | bytes 13500416 | tf_op jit(solution)/shard_map/dot_general | solution.py:8
  174.2 0.0 slice-start.2
  174.2 6.6 %fusion = bf16[1536,4096]{0,1:T(8,128)(2,1)} fusion(bf16[64,4096]{1,0:T(8,128)(2,1)S(1)} %get-tuple-element.15, bf16[64,1536]{1,0:T(8,128)(2,1)S(1)} %all_gather.6), kind=kOutput, calls=%fused_computation.3 | convolution fusion | flops 811597824 | bytes 13303808 | tf_op jit(solution)/shard_map/dot_general | solution.py:14
  180.8 0.0 slice-done
  180.8 0.0 slice-done.1
  180.8 0.0 slice-done.2
  180.8 3.0 %convolution_convert_fusion.3 = bf16[64,1536]{1,0:T(8,128)(2,1)} fusion(bf16[64,4096]{1,0:T(8,128)(2,1)S(1)} %get-tuple-element.16, bf16[4096,1536]{1,0:T(8,128)(2,1)S(1)} %bitcast.23), kind=kOutput, calls=%fused_computation.7 | convolution fusion | flops 805404672 | bytes 13303808 | tf_op jit(solution)/shard_map/dot_general | solution.py:39
  183.8 0.0 reduce-scatter.3.cloned.1.call-update
  183.8 0.3 reduce-scatter.5.cloned.1.call-start
  184.1 6.4 %fusion.1 = bf16[1536,4096]{0,1:T(8,128)(2,1)} fusion(bf16[64,4096]{1,0:T(8,128)(2,1)S(1)} %get-tuple-element.14, bf16[64,1536]{1,0:T(8,128)(2,1)S(1)} %all_gather.6), kind=kOutput, calls=%fused_computation.4 | convolution fusion | flops 811597824 | bytes 13303808 | tf_op jit(solution)/shard_map/dot_general | solution.py:14
  190.5 9.2 %fusion.2 = bf16[64,1536]{1,0:T(8,128)(2,1)} fusion(f32[64,1536]{1,0:T(8,128)S(1)} %fusion.6, bf16[64,4096]{1,0:T(8,128)(2,1)S(1)} %get-tuple-element.14, bf16[1536,4096]{1,0:T(8,128)(2,1)} %param.8), kind=kOutput, calls=%fused_computation.6 | convolution fusion | flops 805502976 | bytes 13697024 | tf_op jit(solution)/shard_map/dot_general | solution.py:8
  199.7 0.0 reduce-scatter.5.cloned.1.call-update
  199.7 6.6 %convolution_convert_fusion = bf16[4096,1536]{1,0:T(8,128)(2,1)} fusion(bf16[64,4096]{1,0:T(8,128)(2,1)S(1)} %get-tuple-element.16, bf16[64,1536]{1,0:T(8,128)(2,1)S(1)} %all_gather.7), kind=kOutput, calls=%fused_computation | convolution fusion | flops 811597824 | bytes 13303808 | tf_op jit(solution)/shard_map/dot_general | solution.py:14
  206.3 16.6 %copy.10 = bf16[1536,4096]{1,0:T(8,128)(2,1)} copy(bf16[1536,4096]{0,1:T(8,128)(2,1)} %fusion) | data formatting | bytes 25165824
  222.9 16.6 %copy.11 = bf16[1536,4096]{1,0:T(8,128)(2,1)} copy(bf16[1536,4096]{0,1:T(8,128)(2,1)} %fusion.1) | data formatting | bytes 25165824
  239.5 0.0 reduce-scatter.3.cloned.1.call-done
  239.5 0.0 reduce-scatter.5.cloned.1.call-done
  (1 shorter events, 0.0 us)
Async XLA Ops:
  7.2 50.8 %all-reduce.8.cloned.1.call-start = ((), (), s32[]{:S(2)}) async-start(), calls=%async_computation.5 | async-start | bytes 4194304 | tf_op jit(solution)/shard_map/psum | solution.py:36
  7.2 23.7 %copy-start = (bf16[1536,4096]{1,0:T(8,128)(2,1)S(1)}, bf16[1536,4096]{1,0:T(8,128)(2,1)}, u32[]{:S(2)}) copy-start(bf16[1536,4096]{1,0:T(8,128)(2,1)} %param.7) | copy-start | bytes 37748740
  30.9 3.3 %copy-start.1 = (bf16[16,1536]{1,0:T(8,128)(2,1)S(1)}, bf16[16,1536]{1,0:T(8,128)(2,1)}, u32[]{:S(2)}) copy-start(bf16[16,1536]{1,0:T(8,128)(2,1)} %param.6) | copy-start | bytes 147460
  34.2 63.1 %all-reduce.6.cloned.1.call-start = ((), (), s32[]{:S(2)}) async-start(), calls=%async_computation.3 | async-start | bytes 2097152 | tf_op jit(solution)/shard_map/psum | solution.py:47
  57.9 105.2 %all-reduce.10.cloned.1.call-start = ((), (), s32[]{:S(2)}) async-start(), calls=%async_computation.6 | async-start | bytes 4194304 | tf_op jit(solution)/shard_map/psum | solution.py:36
  58.7 180.9 %reduce-scatter.3.cloned.1.call-start = ((), (), s32[]{:S(2)}) async-start(), calls=%async_computation.2 | async-start | bytes 245760 | tf_op jit(solution)/shard_map/reduce_scatter | solution.py:38
  165.5 15.3 %slice-start = ((s8[12582912]{0:T(1024)(128)(4,1)}), s8[4194304]{0:T(1024)(128)(4,1)S(1)}, s32[]{:S(2)}) async-start(s8[12582912]{0:T(1024)(128)(4,1)} %bitcast.22), calls=%async_computation.7 | async-start | bytes 8388608
  165.5 15.3 %slice-start.1 = ((s8[12582912]{0:T(1024)(128)(4,1)}), s8[4194304]{0:T(1024)(128)(4,1)S(1)}, s32[]{:S(2)}) async-start(s8[12582912]{0:T(1024)(128)(4,1)} %bitcast.22), calls=%async_computation.8 | async-start | bytes 8388608
  174.2 6.6 %slice-start.2 = ((s8[12582912]{0:T(1024)(128)(4,1)}), s8[4194304]{0:T(1024)(128)(4,1)S(1)}, s32[]{:S(2)}) async-start(s8[12582912]{0:T(1024)(128)(4,1)} %bitcast.22), calls=%async_computation.9 | async-start | bytes 8388608
  183.8 55.7 %reduce-scatter.5.cloned.1.call-start = ((), (), s32[]{:S(2)}) async-start(), calls=%async_computation.4 | async-start | bytes 245760 | tf_op jit(solution)/shard_map/reduce_scatter | solution.py:49
Sparse Core Ops, SparseCore 0:
  34.3 22.6 all-reduce.7
  60.0 37.1 all-reduce.5
  99.6 63.4 all-reduce.9
  183.9 19.3 reduce-scatter.2
  206.0 17.5 reduce-scatter.4
